TPU v7x, 32 devices: a whole 2x2x4 slice. The times are simulated.
32 devices in a mesh: row: 8 (over y, x, core), col: 4 (over z).
Axes of the slice: x: 2, y: 2, z: 4, core: 2. Of those that a mesh axis runs over, the one named last changes fastest.
Arguments:
- sparse_tiles: bfloat16 [128, 7, 128, 128], P(('row', 'col')), may hold values from -0.125 to 0.125
- tile_columns: int32 [128, 7], P(('row', 'col')), may hold values from 0 to 7, as said below
- block_counts: int32 [128], P(('row', 'col')), may hold values from 1 to 7, as said below
- krylov_first: bfloat16 [4096, 256], P(('row', 'col')), may hold values from -6 to 6
- panel_block: bfloat16 [4096, 256], P(('row', 'col')), may hold values from -1 to 1
Outputs:
- triangle_factor: float32 [256, 256], replicated
- coefficients: float32 [256, 768], replicated
- projected: bfloat16 [4096, 768], P(('row', 'col'))
Inputs may be any that keep to these rules, and one draw needn't show every extreme that they name: `tile_columns`: distinct along the last dimension. `block_counts`: some aligned block of 4 entries holds 7 in every entry.
All inputs are finite; a program needn't handle non-finite values.
Results may differ from a plain program's by a relative error of at most 0.0049.
Values may be sent and summed in bfloat16 or wider, within the bound.
A program may use at most 64 MiB of HBM per device.

v0:
```python
import jax
import jax.numpy as jnp
from jax import lax
from jax.sharding import PartitionSpec as P


def factor_small(block):
    order = block.shape[0]
    positions = lax.broadcasted_iota(jnp.int32, (order,), 0)

    def one_column(index, state):
        working, lower, inverse = state
        column = lax.dynamic_slice_in_dim(working, index, 1, 1)[:, 0]
        pivot = jnp.sqrt(lax.dynamic_slice_in_dim(column, index, 1, 0)[0])
        column = jnp.where(positions >= index, column / pivot, jnp.zeros((), column.dtype))
        lower = lax.dynamic_update_slice_in_dim(lower, column[:, None], index, 1)
        working = working - column[:, None] * column[None, :]
        new_row = lax.dynamic_slice_in_dim(inverse, index, 1, 0) / pivot
        below = jnp.where(positions > index, column, jnp.zeros((), column.dtype))
        inverse = inverse - below[:, None] * new_row
        inverse = lax.dynamic_update_slice_in_dim(inverse, new_row, index, 0)
        return (working, lower, inverse)

    start = (block, jnp.zeros_like(block), jnp.eye(order, dtype=block.dtype))
    _, lower, inverse = lax.fori_loop(0, order, one_column, start)
    return (lower, inverse)


def factor_panel(gram_matrix):
    order = gram_matrix.shape[0]
    width = order // 4
    working = gram_matrix
    column_blocks = []
    diag_inverses = []
    for block_index in range(4):
        low = block_index * width
        lower_diag, inverse_diag = factor_small(working[:width, :width])
        under = jnp.dot(working[width:, :width], inverse_diag.T, precision=lax.Precision.HIGHEST)
        working = working[width:, width:] - jnp.dot(under, under.T, precision=lax.Precision.HIGHEST)
        column_blocks.append(
            jnp.concatenate([jnp.zeros((low, width), gram_matrix.dtype), lower_diag, under], axis=0)
        )
        diag_inverses.append(inverse_diag)
    lower = jnp.concatenate(column_blocks, axis=1)
    identity = jnp.eye(order, dtype=gram_matrix.dtype)
    inverse_rows = []
    for block_index in range(4):
        low = block_index * width
        high = low + width
        target = identity[low:high, :]
        if block_index > 0:
            earlier = jnp.concatenate(inverse_rows, axis=0)
            target = target - jnp.dot(
                lower[low:high, :low], earlier, precision=lax.Precision.HIGHEST
            )
        inverse_rows.append(
            jnp.dot(diag_inverses[block_index], target, precision=lax.Precision.HIGHEST)
        )
    return (lower, jnp.concatenate(inverse_rows, axis=0))


def multiply(source, sparse_tiles, tile_columns, block_counts):
    gathered = lax.all_gather(source, "row", axis=0, tiled=True)
    columns = gathered.shape[1]
    tile_size = sparse_tiles.shape[2]
    blocks = gathered.reshape(-1, tile_size, columns)
    picked = jnp.take(blocks, tile_columns, axis=0)
    active = lax.broadcasted_iota(jnp.int32, tile_columns.shape, 1) < block_counts[:, None]
    picked = jnp.where(active[:, :, None, None], picked, jnp.zeros((), picked.dtype))
    partial_value = jnp.einsum(
        "bkij,bkjw->biw", sparse_tiles, picked, preferred_element_type=jnp.float32
    )
    partial_value = partial_value.reshape(-1, columns)
    summed = lax.psum_scatter(partial_value, "col", scatter_dimension=0, tiled=True)
    return summed.astype(jnp.bfloat16)


def inner_products(left, right):
    return jnp.einsum("rp,rq->pq", left, right, preferred_element_type=jnp.float32)


def apply_inverse(lower_inverse, right):
    return jnp.dot(lower_inverse, right, precision=lax.Precision.HIGHEST)


def shards(sparse_tiles, tile_columns, block_counts, krylov_first, panel_block):
    gram_local = inner_products(panel_block, panel_block)
    krylov_second = multiply(krylov_first, sparse_tiles, tile_columns, block_counts)
    krylov_third = multiply(krylov_second, sparse_tiles, tile_columns, block_counts)
    trailing = jnp.concatenate([krylov_first, krylov_second, krylov_third], axis=1)
    gram_matrix, cross_terms = lax.psum(
        (gram_local, inner_products(panel_block, trailing)), ("row", "col")
    )
    lower_factor, lower_inverse = factor_panel(gram_matrix)
    coefficients = apply_inverse(lower_inverse, cross_terms)
    weights = jnp.dot(lower_inverse.T, coefficients, precision=lax.Precision.HIGHEST)
    weight_high = weights.astype(jnp.bfloat16)
    weight_rest = (weights - weight_high.astype(jnp.float32)).astype(jnp.bfloat16)
    removed = jnp.dot(panel_block, weight_high, preferred_element_type=jnp.float32)
    removed = removed + jnp.dot(panel_block, weight_rest, preferred_element_type=jnp.float32)
    projected = (trailing.astype(jnp.float32) - removed).astype(jnp.bfloat16)
    return (lower_factor.T, coefficients, projected)


def solution(mesh):
    in_specs = (
        P(("row", "col"), None, None, None),
        P(("row", "col"), None),
        P(("row", "col")),
        P(("row", "col"), None),
        P(("row", "col"), None),
    )
    out_specs = (P(), P(), P(("row", "col"), None))
    return jax.shard_map(shards, mesh=mesh, in_specs=in_specs, out_specs=out_specs, check_vma=False)
```

profile of v0, /device:TPU:0, one launch (start us, length us, event | category | flops | bytes accessed | tf_op | source)
XLA Modules:
  0.0 632.4 jit_solution(11526809031231209249)
XLA Ops:
  7.2 0.8 compare_select_fusion.4
  8.0 0.8 iota_compare_fusion.3
  8.8 11.6 %all_gather.6 = bf16[1024,256]{1,0:T(8,128)(2,1)S(1)} all-gather(bf16[128,256]{1,0:T(8,128)(2,1)} %param.18), channel_id=1, replica_groups=mesh['row'=8,'col'=4] {'row'}, dimensions={0}, use_global_device_ids=true | all-gather | bytes 589824 | tf_op jit(solution)/shard_map/all_gather | solution.py:63
  20.5 0.7 gather_fusion
  21.7 1.0 copy.23
  22.8 22.2 %reduce-scatter.3.cloned.1.call-done = f32[128,256]{0,1:T(8,128)} async-done(((f32[512,256]{0,1:T(8,128)}), f32[128,256]{0,1:T(8,128)}) %reduce-scatter.3.cloned.1.call-update) | async-done | bytes 131088 | tf_op jit(solution)/shard_map/reduce_scatter | solution.py:74
  45.0 0.9 convert_element_type.42
  45.9 9.9 %all_gather.7 = bf16[1024,256]{0,1:T(8,128)(2,1)S(1)} all-gather(bf16[128,256]{0,1:T(8,128)(2,1)S(1)} %convert_element_type.42), channel_id=1, replica_groups=mesh['row'=8,'col'=4] {'row'}, dimensions={0}, use_global_device_ids=true | all-gather | bytes 589824 | tf_op jit(solution)/shard_map/all_gather | solution.py:63
  56.0 0.7 gather_fusion.1
  57.2 1.0 copy.25
  58.4 0.9 fusion.70
  59.3 18.3 %reduce-scatter.5.cloned.1.call-done = f32[128,256]{0,1:T(8,128)} async-done(((f32[512,256]{0,1:T(8,128)}), f32[128,256]{0,1:T(8,128)}) %reduce-scatter.5.cloned.1.call-update) | async-done | bytes 131088 | tf_op jit(solution)/shard_map/reduce_scatter | solution.py:74
  77.6 0.9 convert_element_type.43
  78.6 1.1 convolution_bitcast_fusion
  79.8 133.0 %all-reduce.4.cloned.1.call-done = (f32[256,256]{1,0:T(8,128)}, f32[256,768]{0,1:T(8,128)}) async-done(((f32[256,256]{1,0:T(8,128)}, f32[256,768]{0,1:T(8,128)}), (f32[256,256]{1,0:T(8,128)}, f32[256,768]{0,1:T(8,128)})) %all-reduce.4.cloned.1.call-update) | async-done | bytes 1048592 | tf_op jit(solution)/shard_map/psum | solution.py:91
  212.8 0.8 slice.70
  213.6 100.6 %while.88 = (s32[]{:T(128)}, f32[64,64]{0,1:T(8,128)S(1)}, f32[64,64]{0,1:T(8,128)S(1)}, f32[64,64]{1,0:T(8,128)S(1)}, s32[]{:T(128)}, /*index=5*/s32[]{:T(128)}, s32[]{:T(128)}) while((s32[]{:T(128)}, f32[64,64]{0,1:T(8,128)S(1)}, f32[64,64]{0,1:T(8,128)S(1)}, f32[64,64]{1,0:T(8,128)S(1)}, s32[]{:T(128)}, ...), condition=%wide.region_2.3_spmd.clone.clone, body=%wide.region_1.2_spmd.clone.clone.sunk | while | flops 16963 | bytes 71821 | solution.py:25
  213.7 0.6 dynamic_slice.166
  215.2 0.6 dynamic_slice.166
  216.8 0.6 dynamic_slice.166
  218.4 0.6 dynamic_slice.166
  219.9 0.6 dynamic_slice.166
  221.5 0.6 dynamic_slice.166
  246.6 0.6 dynamic_slice.166
  271.8 0.6 dynamic_slice.166
  298.5 0.6 dynamic_slice.166
  314.3 1.2 fusion.46
  315.7 1.3 convolution_subtract_fusion
  317.1 100.6 %while.89 = (s32[]{:T(128)}, f32[64,64]{0,1:T(8,128)S(1)}, f32[64,64]{0,1:T(8,128)S(1)}, f32[64,64]{1,0:T(8,128)S(1)}, s32[]{:T(128)}, /*index=5*/s32[]{:T(128)}, s32[]{:T(128)}) while((s32[]{:T(128)}, f32[64,64]{0,1:T(8,128)S(1)}, f32[64,64]{0,1:T(8,128)S(1)}, f32[64,64]{1,0:T(8,128)S(1)}, s32[]{:T(128)}, ...), condition=%wide.region_4.5_spmd.clone.clone, body=%wide.region_3.4_spmd.clone.clone.sunk | while | flops 16963 | bytes 71821 | solution.py:25
  328.1 0.6 dynamic_slice.169
  339.1 0.6 dynamic_slice.169
  367.4 0.6 dynamic_slice.169
  403.5 0.6 dynamic_slice.169
  418.8 100.7 %while.90 = (s32[]{:T(128)}, f32[64,64]{0,1:T(8,128)S(1)}, f32[64,64]{0,1:T(8,128)S(1)}, f32[64,64]{1,0:T(8,128)S(1)}, s32[]{:T(128)}, /*index=5*/s32[]{:T(128)}, s32[]{:T(128)}) while((s32[]{:T(128)}, f32[64,64]{0,1:T(8,128)S(1)}, f32[64,64]{0,1:T(8,128)S(1)}, f32[64,64]{1,0:T(8,128)S(1)}, s32[]{:T(128)}, ...), condition=%wide.region_6.7_spmd.clone.clone, body=%wide.region_5.6_spmd.clone.clone.sunk | while | flops 16963 | bytes 71821 | solution.py:25
  429.8 0.6 dynamic_slice.172
  447.1 0.6 dynamic_slice.172
  484.9 0.6 dynamic_slice.172
  506.9 0.6 dynamic_slice.172
  520.6 100.6 %while.91 = (s32[]{:T(128)}, f32[64,64]{0,1:T(8,128)S(1)}, f32[64,64]{0,1:T(8,128)S(1)}, f32[64,64]{1,0:T(8,128)S(1)}, s32[]{:T(128)}, /*index=5*/s32[]{:T(128)}, s32[]{:T(128)}) while((s32[]{:T(128)}, f32[64,64]{0,1:T(8,128)S(1)}, f32[64,64]{0,1:T(8,128)S(1)}, f32[64,64]{1,0:T(8,128)S(1)}, s32[]{:T(128)}, ...), condition=%wide.region_8.9_spmd.clone.clone, body=%wide.region_7.8_spmd.clone.clone.sunk | while | flops 16963 | bytes 71821 | solution.py:25
  526.9 0.6 dynamic_slice.175
  541.0 0.6 dynamic_slice.175
  569.3 0.6 dynamic_slice.175
  585.0 0.6 dynamic_slice.175
  610.2 0.6 dynamic_slice.175
  621.9 0.8 fusion.35
  622.7 0.8 fusion.34
  624.2 0.8 copy.27
  625.0 0.8 fusion.25
  (2335 shorter events, 206.8 us)
Async XLA Ops:
  7.2 14.0 %copy-start = (bf16[4,7,128,128]{3,2,1,0:T(8,128)(2,1)S(1)}, bf16[4,7,128,128]{3,2,1,0:T(8,128)(2,1)}, u32[]{:S(2)}) copy-start(bf16[4,7,128,128]{3,2,1,0:T(8,128)(2,1)} %param.15) | copy-start | bytes 2752516
  7.2 37.8 %reduce-scatter.3.cloned.1.call-start = ((), (), s32[]{:S(2)}) async-start(), calls=%async_computation.2 | async-start | bytes 655360 | tf_op jit(solution)/shard_map/reduce_scatter | solution.py:74
  22.7 54.9 %reduce-scatter.5.cloned.1.call-start = ((), (), s32[]{:S(2)}) async-start(), calls=%async_computation.3 | async-start | bytes 655360 | tf_op jit(solution)/shard_map/reduce_scatter | solution.py:74
  56.6 1.7 copy-start.4
  56.6 1.8 copy-start.2
  58.2 154.6 %all-reduce.4.cloned.1.call-start = ((), (), s32[]{:S(2)}) async-start(), calls=%async_computation.4 | async-start | bytes 2097152 | tf_op jit(solution)/shard_map/psum | solution.py:91
  418.8 203.0 %copy-start.3 = (f32[256,768]{0,1:T(8,128)S(1)}, f32[256,768]{0,1:T(8,128)}, u32[]{:S(2)}) copy-start(f32[256,768]{0,1:T(8,128)} %get-tuple-element.787) | copy-start | bytes 2359300
  622.7 1.5 copy-start.1
Sparse Core Ops, SparseCore 0:
  22.8 22.0 reduce-scatter.2
  58.4 19.2 reduce-scatter.4
  83.6 129.1 all-reduce.3
where the time goes:
time: 635 us; the launch traced here: 632 us
  loops' own time  188 us (30%)
  waiting for transfers between devices  174 us (27%)
  local copies, waits for them, and re-layouts  170 us (27%)
  other arithmetic  54.3 us (9%)
  blocking collectives  21.5 us (3%)
  between operations  14.1 us (2%)
  matrix products  10.6 us (2%)
    another operation x4, loops' own time, factor_small(): _, lower, inverse = lax.fori_loop(0, order, one_column, start)  188 us
    dynamic_slice x256, local copies, waits for them, and re-layouts, one_column(): pivot = jnp.sqrt(lax.dynamic_slice_in_dim(column, index, 1, 0)[0])  151 us
    psum x1, waiting for transfers between devices, shards(): lax.psum((gram_local, inner_products(panel_block, trailing)), ('row', 'co...  133 us
    reduce_scatter x2, waiting for transfers between devices, multiply(): lax.psum_scatter(partial_value, 'col', scatter_dimension=0, tiled=True)  40.5 us
    all_gather x2, blocking collectives, multiply(): gathered = lax.all_gather(source, 'row', axis=0, tiled=True)  21.5 us
    sub x256, other arithmetic, one_column(): working = working - column[:, None] * column[None, :]  19.4 us
    sub x256, other arithmetic, one_column(): inverse = inverse - below[:, None] * new_row  19.3 us
  transfers between devices with their start and end apart: 3, of which 3 were waited for; matrix products, arithmetic and copies ran while one was open for 0% of the time, Pallas kernels for 0%

commit v1 on v0

v1 whole, which is shorter than its diff:
```python
import functools

import jax
import jax.numpy as jnp
from jax import lax
from jax.experimental import pallas as pl
from jax.experimental.pallas import tpu as pltpu
from jax.sharding import PartitionSpec as P

HIGHEST = lax.Precision.HIGHEST
F32 = jnp.float32
BF16 = jnp.bfloat16


def dot_nn(a, b, precision=None):
    return lax.dot_general(a, b, (((1,), (0,)), ((), ())), precision=precision, preferred_element_type=F32)


def dot_nt(a, b, precision=None):
    return lax.dot_general(a, b, (((1,), (1,)), ((), ())), precision=precision, preferred_element_type=F32)


def dot_tn(a, b, precision=None):
    return lax.dot_general(a, b, (((0,), (0,)), ((), ())), precision=precision, preferred_element_type=F32)


def eliminate(diag, work_ref, out_ref):
    width = diag.shape[0]
    low = lax.broadcasted_iota(jnp.int32, (width, width), 0)
    high = lax.broadcasted_iota(jnp.int32, (width, width), 1)
    work_ref[...] = jnp.concatenate([diag, (low == high).astype(F32)], axis=1)
    sub = lax.broadcasted_iota(jnp.int32, (8, 2 * width), 0)

    def group(index, carry):
        rows = work_ref[:8, :]
        scale = jnp.zeros((8, 2 * width), F32)
        spread = [jnp.broadcast_to(rows[:, k : k + 1], (8, 2 * width)) for k in range(8)]
        for i in range(8):
            inverse = 1.0 / jnp.broadcast_to(spread[i][i : i + 1, :], (8, 2 * width))
            factor = jnp.where(sub > i, spread[i] * inverse, 0.0)
            scale = jnp.where(sub == i, inverse, scale)
            for k in range(i + 1, 8):
                spread[k] = spread[k] - factor * spread[k][i : i + 1, :]
            rows = rows - factor * rows[i : i + 1, :]
        scaled = rows * scale
        rest = work_ref[...] - dot_tn(scaled[:, :width], rows, HIGHEST)
        at = pl.multiple_of(index * 8, 8)
        out_ref[pl.ds(at, 8), :] = pltpu.roll(rows * jnp.sqrt(scale), index * 8, 1)
        rest = pltpu.roll(rest, 2 * width - 8, 1)
        work_ref[: width - 8, :] = rest[8:, :]
        work_ref[width - 8 :, :] = jnp.zeros((8, 2 * width), F32)
        return carry

    lax.fori_loop(0, width // 8, group, 0)
    both = out_ref[...]
    upper = jnp.where(high >= low, both[:, :width], 0.0)
    inverse = jnp.where(high <= low, both[:, width:], 0.0)
    return upper, inverse


def body(n_row, n_col, degree, row_blocks, tile,
         tiles_hbm, columns_ref, counts_ref, first_ref, panel_ref,
         upper_out, coef_out, proj_out,
         tiles_ref, gathered_a, gathered_b, sums_ref, send_a, send_b, get_a, get_b,
         second_ref, third_ref,
         part_0, part_1, part_2, take_0, take_1, take_2,
         mix_0, mix_1, mix_2, full_0, full_1, full_2,
         work_ref, out_ref, lower_ref,
         tile_sem, gs_sem, gr_sem, ss_sem, sr_sem, rs_sem, rr_sem, xs_sem, xr_sem, as_sem, ar_sem):
    row = lax.axis_index("row")
    col = lax.axis_index("col")
    panel_width = panel_ref.shape[1]
    rows_dev = panel_ref.shape[0]
    strip = panel_width // n_row

    load_tiles = pltpu.make_async_copy(tiles_hbm, tiles_ref, tile_sem)
    load_tiles.start()

    def row_peer(step):
        return lax.rem(row + step, n_row)

    def col_peer(step):
        return lax.rem(col + step, n_col)

    barrier = pltpu.get_barrier_semaphore()
    for step in range(1, n_row):
        pl.semaphore_signal(barrier, inc=1, device_id=(row_peer(step), col), device_id_type=pl.DeviceIdType.MESH)
    for step in range(1, n_col):
        pl.semaphore_signal(barrier, inc=1, device_id=(row, col_peer(step)), device_id_type=pl.DeviceIdType.MESH)

    def over_row(source, target, send_sem, recv_sem):
        copies = []
        for step in range(1, n_row):
            peer = row_peer(step)
            copies.append(pltpu.make_async_remote_copy(
                src_ref=source(step, peer), dst_ref=target(step, peer),
                send_sem=send_sem.at[step], recv_sem=recv_sem.at[step],
                device_id=(peer, col), device_id_type=pl.DeviceIdType.MESH))
        return copies

    def over_col(source, target, send_sem, recv_sem):
        copies = []
        for step in range(1, n_col):
            peer = col_peer(step)
            copies.append(pltpu.make_async_remote_copy(
                src_ref=source(step, peer), dst_ref=target(step, peer),
                send_sem=send_sem.at[step], recv_sem=recv_sem.at[step],
                device_id=(row, peer), device_id_type=pl.DeviceIdType.MESH))
        return copies

    def start(copies):
        for copy in copies:
            copy.start()

    def arrive(copies):
        for copy in copies:
            copy.wait_recv()

    def gather(source_ref, gathered_ref, index):
        copies = over_row(lambda s, p: source_ref, lambda s, p: gathered_ref.at[row],
                          gs_sem.at[index], gr_sem.at[index])
        start(copies)
        gathered_ref[row] = source_ref[...]
        return copies

    def product(gathered_ref, send_ref):
        for b in range(row_blocks):
            left, right = [], []
            for k in range(degree):
                live = k < counts_ref[0, b]
                value = tiles_ref[b, k]
                left.append(jnp.where(live, value, jnp.zeros_like(value)))
                right.append(gathered_ref[columns_ref[b, k]])
            total = dot_nn(jnp.concatenate(left, axis=1), jnp.concatenate(right, axis=0))
            sums_ref[b * tile : (b + 1) * tile, :] = total
        for c in range(n_col):
            send_ref[c] = sums_ref[c * rows_dev : (c + 1) * rows_dev, :].astype(BF16)

    def scatter(send_ref, get_ref, index):
        copies = over_col(lambda s, p: send_ref.at[p], lambda s, p: get_ref.at[s],
                          ss_sem.at[index], sr_sem.at[index])
        start(copies)
        return copies

    def collect(copies, get_ref, result_ref):
        own = sums_ref[pl.ds(pl.multiple_of(col * rows_dev, 8), rows_dev), :]
        arrive(copies)
        for step in range(1, n_col):
            own = own + get_ref[step].astype(F32)
        result_ref[...] = own.astype(BF16)

    def reduce_row(value_parts, part_ref, take_ref, index):
        at = 0
        for value in value_parts:
            width = value.shape[1]
            part_ref[:, :, at : at + width] = value.reshape(n_row, strip, width)
            at += width
        copies = over_row(lambda s, p: part_ref.at[p], lambda s, p: take_ref.at[s],
                          rs_sem.at[index], rr_sem.at[index])
        start(copies)
        return copies

    def exchange_col(copies, part_ref, take_ref, mix_ref, index):
        total = part_ref[row]
        arrive(copies)
        for step in range(1, n_row):
            total = total + take_ref[step]
        mix_ref[col] = total
        copies = over_col(lambda s, p: mix_ref.at[col], lambda s, p: mix_ref.at[col],
                          xs_sem.at[index], xr_sem.at[index])
        start(copies)
        return copies

    def share_row(copies, mix_ref, full_ref, index):
        arrive(copies)
        total = mix_ref[0]
        for c in range(1, n_col):
            total = total + mix_ref[c]
        full_ref[row] = total
        copies = over_row(lambda s, p: full_ref.at[row], lambda s, p: full_ref.at[row],
                          as_sem.at[index], ar_sem.at[index])
        start(copies)
        return copies

    panel = panel_ref[...]
    gram_local = dot_tn(panel, panel)
    pl.semaphore_wait(barrier, n_row - 1 + n_col - 1)

    sent = []
    reduce_0 = reduce_row([gram_local], part_0, take_0, 0)
    gather_1 = gather(first_ref, gathered_a, 0)
    first_local = dot_tn(panel, first_ref[...])
    exchange_0 = exchange_col(reduce_0, part_0, take_0, mix_0, 0)
    load_tiles.wait()
    arrive(gather_1)
    product(gathered_a, send_a)
    scatter_1 = scatter(send_a, get_a, 0)
    share_0 = share_row(exchange_0, mix_0, full_0, 0)
    collect(scatter_1, get_a, second_ref)
    gather_2 = gather(second_ref, gathered_b, 1)
    reduce_1 = reduce_row([first_local, dot_tn(panel, second_ref[...])], part_1, take_1, 1)
    arrive(share_0)
    gram = full_0[...].reshape(panel_width, panel_width)
    pieces = 4
    width = panel_width // pieces
    columns = [gram[width * j :, width * j : width * (j + 1)] for j in range(pieces)]
    uppers, inverses, unders = [], [], []

    def factor(b):
        upper, inverse = eliminate(columns[b][:width], work_ref, out_ref)
        under = None
        if b < pieces - 1:
            under = dot_nt(columns[b][width:], inverse, HIGHEST)
            for j in range(b + 1, pieces):
                o = (j - b - 1) * width
                columns[j] = columns[j] - dot_nt(under[o:], under[o : o + width], HIGHEST)
        uppers.append(upper)
        inverses.append(inverse)
        unders.append(under)

    arrive(gather_2)
    product(gathered_b, send_b)
    scatter_2 = scatter(send_b, get_b, 1)
    exchange_1 = exchange_col(reduce_1, part_1, take_1, mix_1, 1)
    factor(0)
    collect(scatter_2, get_b, third_ref)
    reduce_2 = reduce_row([dot_tn(panel, third_ref[...])], part_2, take_2, 2)
    share_1 = share_row(exchange_1, mix_1, full_1, 1)
    factor(1)
    exchange_2 = exchange_col(reduce_2, part_2, take_2, mix_2, 2)
    factor(2)
    share_2 = share_row(exchange_2, mix_2, full_2, 2)
    factor(3)

    identity = (lax.broadcasted_iota(jnp.int32, (width, panel_width), 1)
                - lax.broadcasted_iota(jnp.int32, (width, panel_width), 0))
    for b in range(pieces):
        target = (identity == b * width).astype(F32)
        for e in range(b):
            o = (b - e - 1) * width
            target = target - dot_nn(unders[e][o : o + width], lower_ref[e * width : (e + 1) * width, :], HIGHEST)
        lower_ref[b * width : (b + 1) * width, :] = dot_nn(inverses[b], target, HIGHEST)
    for b in range(pieces):
        parts = [jnp.zeros((width, b * width), F32)] if b else []
        parts.append(uppers[b])
        if b < pieces - 1:
            parts.append(unders[b].T)
        upper_out[b * width : (b + 1) * width, :] = jnp.concatenate(parts, axis=1)

    def finish(full_ref, sources, at):
        lower_inverse = lower_ref[...]
        cross = full_ref[...].reshape(panel_width, full_ref.shape[2])
        coefficients = dot_nn(lower_inverse, cross, HIGHEST)
        coef_out[:, at : at + cross.shape[1]] = coefficients
        weights = dot_tn(lower_inverse, coefficients, HIGHEST)
        weight_high = weights.astype(BF16)
        weight_rest = (weights - weight_high.astype(F32)).astype(BF16)
        removed = dot_nn(panel_ref[...], weight_high) + dot_nn(panel_ref[...], weight_rest)
        for j, source in enumerate(sources):
            here = removed[:, j * panel_width : (j + 1) * panel_width]
            low = at + j * panel_width
            proj_out[:, low : low + panel_width] = (source[...].astype(F32) - here).astype(BF16)

    arrive(share_1)
    finish(full_1, [first_ref, second_ref], 0)
    arrive(share_2)
    finish(full_2, [third_ref], 2 * panel_width)

    for copies in (reduce_0, gather_1, exchange_0, scatter_1, share_0, gather_2, reduce_1, scatter_2,
                   exchange_1, reduce_2, share_1, exchange_2, share_2):
        for copy in copies:
            copy.wait_send()


def shards(n_row, n_col, sparse_tiles, tile_columns, block_counts, krylov_first, panel_block):
    row_blocks, degree, tile, _ = sparse_tiles.shape
    rows_dev, width = panel_block.shape
    strip = width // n_row
    vmem = pl.BlockSpec(memory_space=pltpu.VMEM)
    smem = pl.BlockSpec(memory_space=pltpu.SMEM)
    call = pl.pallas_call(
        functools.partial(body, n_row, n_col, degree, row_blocks, tile),
        out_shape=[
            jax.ShapeDtypeStruct((width, width), F32),
            jax.ShapeDtypeStruct((width, 3 * width), F32),
            jax.ShapeDtypeStruct((rows_dev, 3 * width), BF16),
        ],
        in_specs=[pl.BlockSpec(memory_space=pl.ANY), smem, smem, vmem, vmem],
        out_specs=[vmem, vmem, vmem],
        scratch_shapes=[
            pltpu.VMEM(sparse_tiles.shape, BF16),
            pltpu.VMEM((n_row, rows_dev, width), BF16),
            pltpu.VMEM((n_row, rows_dev, width), BF16),
            pltpu.VMEM((row_blocks * tile, width), F32),
            pltpu.VMEM((n_col, rows_dev, width), BF16),
            pltpu.VMEM((n_col, rows_dev, width), BF16),
            pltpu.VMEM((n_col, rows_dev, width), BF16),
            pltpu.VMEM((n_col, rows_dev, width), BF16),
            pltpu.VMEM((rows_dev, width), BF16),
            pltpu.VMEM((rows_dev, width), BF16),
            *[pltpu.VMEM((n_row, strip, k * width), F32) for k in (1, 2, 1)],
            *[pltpu.VMEM((n_row, strip, k * width), F32) for k in (1, 2, 1)],
            *[pltpu.VMEM((n_col, strip, k * width), F32) for k in (1, 2, 1)],
            *[pltpu.VMEM((n_row, strip, k * width), F32) for k in (1, 2, 1)],
            pltpu.VMEM((width // 4, width // 2), F32),
            pltpu.VMEM((width // 4, width // 2), F32),
            pltpu.VMEM((width, width), F32),
            pltpu.SemaphoreType.DMA,
            *[pltpu.SemaphoreType.DMA((2, n_row))] * 2,
            *[pltpu.SemaphoreType.DMA((2, n_col))] * 2,
            *[pltpu.SemaphoreType.DMA((3, n_row))] * 2,
            *[pltpu.SemaphoreType.DMA((3, n_col))] * 2,
            *[pltpu.SemaphoreType.DMA((3, n_row))] * 2,
        ],
        compiler_params=pltpu.CompilerParams(collective_id=0, has_side_effects=True),
        name="range_finder",
    )
    return tuple(call(sparse_tiles, tile_columns, block_counts.reshape(1, row_blocks), krylov_first, panel_block))


def solution(mesh):
    n_row, n_col = mesh.shape["row"], mesh.shape["col"]
    in_specs = (
        P(("row", "col"), None, None, None),
        P(("row", "col"), None),
        P(("row", "col")),
        P(("row", "col"), None),
        P(("row", "col"), None),
    )
    out_specs = (P(), P(), P(("row", "col"), None))
    return jax.shard_map(
        functools.partial(shards, n_row, n_col), mesh=mesh, in_specs=in_specs, out_specs=out_specs, check_vma=False
    )
```

time: 635 us -> 70.1 us (0.11)
  loops' own time: 188 us -> 0 us
  waiting for transfers between devices: 174 us -> 0 us
  local copies, waits for them, and re-layouts: 170 us -> 4.45 us
  Pallas kernels: 0 us -> 64.8 us
  other arithmetic: 54.3 us -> 0 us
  blocking collectives: 21.5 us -> 0 us
  between operations: 14.1 us -> 0.64 us
  matrix products: 10.6 us -> 0 us
    another operation x4 -> x0, loops' own time: 188 us -> none  [factor_small(): _, lower, inverse = lax.fori_loop(0, order, one_column, start)]
    dynamic_slice x256 -> x0, local copies, waits for them, and re-layouts: 151 us -> none  [one_column(): pivot = jnp.sqrt(lax.dynamic_slice_in_dim(column, index, 1, 0)[0])]
    psum x1 -> x0, waiting for transfers between devices: 133 us -> none  [shards(): lax.psum((gram_local, inner_products(panel_block, trailing)), ('row', 'co...]
    pallas_call x0 -> x1, Pallas kernels: none -> 64.8 us  [shards(): call(sparse_tiles, tile_columns, block_counts.reshape(1, row_blocks), kry...]
    reduce_scatter x2 -> x0, waiting for transfers between devices: 40.5 us -> none  [multiply(): lax.psum_scatter(partial_value, 'col', scatter_dimension=0, tiled=True)]
    sub x512 -> x0, other arithmetic: 38.7 us -> none  [the longest x256 19.4 us: one_column(): working = working - column[:, None] * column[None, :]]
    all_gather x2 -> x0, blocking collectives: 21.5 us -> none  [multiply(): gathered = lax.all_gather(source, 'row', axis=0, tiled=True)]
    dynamic_update_slice x512 -> x0, local copies, waits for them, and re-layouts: 13.7 us -> none  [the longest x256 7.07 us: one_column(): inverse = lax.dynamic_update_slice_in_dim(inverse, new_row, index, 0)]
  transfers between devices with their start and end apart: 3 -> 0, of which waited for: 3 -> 0; matrix products, arithmetic and copies ran while one was open for 0% -> 0% of each run, Pallas kernels for 0% -> 0%
where the time goes in v1:
time: 70.1 us; the launch traced here: 69.8 us
  Pallas kernels  64.8 us (92%)
  local copies, waits for them, and re-layouts  4.45 us (6%)
    pallas_call x1, Pallas kernels, shards(): call(sparse_tiles, tile_columns, block_counts.reshape(1, row_blocks), kry...  64.8 us
    unnamed x5, local copies, waits for them, and re-layouts  4.45 us

profile of v1, /device:TPU:0, one launch (start us, length us, event | category | flops | bytes accessed | tf_op | source)
XLA Modules:
  0.0 69.8 jit_solution(9582005651810622669)
XLA Ops:
  0.6 64.8 %range_finder.1 = (f32[256,256]{1,0:T(8,128)}, f32[256,768]{1,0:T(8,128)}, bf16[128,768]{1,0:T(8,128)(2,1)}) custom-call(bf16[4,7,128,128]{3,2,1,0:T(8,128)(2,1)} %tiles_hbm.1, s32[4,7]{1,0:T(4,128)} %columns_ref.1, s32[1,4]{1,0:T(1,128)} %bitcast.1, bf16[128,256]{1,0:T(8,128)(2,1)} %first_ref.1, bf16[128,256]{1,0:T(8,128)(2,1)} %panel_ref.1), custom_call_target="tpu_custom_call" | custom-call | tf_op jit(solution)/shard_map/range_finder/pallas_call | solution.py:318
  65.4 1.7 %copy.11 = f32[256,256]{1,0:T(8,128)} copy(f32[256,256]{1,0:T(8,128)} %get-tuple-element.6) | data formatting | bytes 524288
  67.1 0.0 copy-start
  67.1 2.1 %copy.12 = f32[256,768]{1,0:T(8,128)} copy(f32[256,768]{1,0:T(8,128)} %get-tuple-element.7) | data formatting | bytes 1572864
  69.2 0.0 copy-done
  69.2 0.7 copy.13
Async XLA Ops:
  67.1 2.1 %copy-start = (bf16[128,768]{1,0:T(8,128)(2,1)S(1)}, bf16[128,768]{1,0:T(8,128)(2,1)}, u32[]{:S(2)}) copy-start(bf16[128,768]{1,0:T(8,128)(2,1)} %get-tuple-element.8) | copy-start | bytes 589828

commit v2 on v1

v2 whole, which is shorter than its diff:
```python
import functools

import jax
import jax.numpy as jnp
from jax import lax
from jax.experimental import pallas as pl
from jax.experimental.pallas import tpu as pltpu
from jax.sharding import PartitionSpec as P

HIGHEST = lax.Precision.HIGHEST
F32 = jnp.float32
BF16 = jnp.bfloat16


def dot_nn(a, b, precision=None):
    return lax.dot_general(a, b, (((1,), (0,)), ((), ())), precision=precision, preferred_element_type=F32)


def dot_nt(a, b, precision=None):
    return lax.dot_general(a, b, (((1,), (1,)), ((), ())), precision=precision, preferred_element_type=F32)


def dot_tn(a, b, precision=None):
    return lax.dot_general(a, b, (((0,), (0,)), ((), ())), precision=precision, preferred_element_type=F32)


def eliminate(diag, work_ref, out_ref):
    width = diag.shape[0]
    low = lax.broadcasted_iota(jnp.int32, (width, width), 0)
    high = lax.broadcasted_iota(jnp.int32, (width, width), 1)
    work_ref[...] = jnp.concatenate([diag, (low == high).astype(F32)], axis=1)
    sub = lax.broadcasted_iota(jnp.int32, (8, 2 * width), 0)

    def group(index, carry):
        rows = work_ref[:8, :]
        scale = jnp.zeros((8, 2 * width), F32)
        spread = [jnp.broadcast_to(rows[:, k : k + 1], (8, 2 * width)) for k in range(8)]
        for i in range(8):
            inverse = 1.0 / jnp.broadcast_to(spread[i][i : i + 1, :], (8, 2 * width))
            factor = jnp.where(sub > i, spread[i] * inverse, 0.0)
            scale = jnp.where(sub == i, inverse, scale)
            for k in range(i + 1, 8):
                spread[k] = spread[k] - factor * spread[k][i : i + 1, :]
            rows = rows - factor * rows[i : i + 1, :]
        scaled = rows * scale
        rest = work_ref[...] - dot_tn(scaled[:, :width], rows, HIGHEST)
        at = pl.multiple_of(index * 8, 8)
        out_ref[pl.ds(at, 8), :] = pltpu.roll(rows * jnp.sqrt(scale), index * 8, 1)
        rest = pltpu.roll(rest, 2 * width - 8, 1)
        work_ref[: width - 8, :] = rest[8:, :]
        work_ref[width - 8 :, :] = jnp.zeros((8, 2 * width), F32)
        return carry

    lax.fori_loop(0, width // 8, group, 0)
    both = out_ref[...]
    upper = jnp.where(high >= low, both[:, :width], 0.0)
    inverse = jnp.where(high <= low, both[:, width:], 0.0)
    return upper, inverse


def over_chunks(total, chunk, run):
    if total <= chunk:
        run(0, total)
    else:
        def one(index, carry):
            run(pl.multiple_of(index * chunk, chunk), chunk)
            return carry

        lax.fori_loop(0, total // chunk, one, 0)


def body(n_row, n_col, degree, row_blocks, tile,
         tiles_hbm, columns_ref, counts_ref, first_ref, panel_ref,
         lower_ref, upper_out, cross_out, second_ref, third_ref,
         tiles_ref, dense_ref, gathered_a, gathered_b, panels_ref, sums_ref, send_a, send_b, get_a, get_b,
         wing_ref, wing_core, wing_half, wing_take, wing_own,
         part_0, part_1, part_2, core_0, core_1, core_2, half_0, half_1, half_2, take_0, take_1, take_2,
         mix_0, mix_1, mix_2, full_0, full_1, full_2,
         work_ref, out_ref,
         tile_sem, gs_sem, gr_sem, gfs_sem, gfr_sem, ps_sem, pr_sem, ss_sem, sr_sem,
         cs_sem, cr_sem, rs_sem, rr_sem, xs_sem, xr_sem, as_sem, ar_sem, afs_sem, afr_sem):
    row = lax.axis_index("row")
    col = lax.axis_index("col")
    panel_width = panel_ref.shape[1]
    rows_dev = panel_ref.shape[0]
    n_chip = n_row // 2
    chip = row // 2
    core = lax.rem(row, 2)
    other = 1 - core
    partner = chip * 2 + other
    mesh_type = pl.DeviceIdType.MESH

    load_tiles = pltpu.make_async_copy(tiles_hbm, tiles_ref, tile_sem)
    load_tiles.start()

    def ahead(step):
        return lax.rem(chip + step, n_chip)

    def behind(step):
        return lax.rem(chip + n_chip - step, n_chip)

    def col_peer(step):
        return lax.rem(col + step, n_col)

    barrier = pltpu.get_barrier_semaphore()
    pl.semaphore_signal(barrier, inc=1, device_id=(partner, col), device_id_type=mesh_type)
    for step in range(1, n_chip):
        pl.semaphore_signal(barrier, inc=1, device_id=(ahead(step) * 2 + core, col), device_id_type=mesh_type)
    for step in range(1, n_col):
        pl.semaphore_signal(barrier, inc=1, device_id=(row, col_peer(step)), device_id_type=mesh_type)

    everything = []

    def begin(copies):
        for copy in copies:
            copy.start()
        everything.extend(copies)
        return copies

    def arrive(copies):
        for copy in copies:
            copy.wait_recv()

    def to_partner(source, target, send_sem, recv_sem):
        return pltpu.make_async_remote_copy(
            src_ref=source, dst_ref=target, send_sem=send_sem, recv_sem=recv_sem,
            device_id=(partner, col), device_id_type=mesh_type)

    def over_chips(source, target, send_sem, recv_sem):
        return [
            pltpu.make_async_remote_copy(
                src_ref=source(step), dst_ref=target(step),
                send_sem=send_sem.at[step], recv_sem=recv_sem.at[step],
                device_id=(ahead(step) * 2 + core, col), device_id_type=mesh_type)
            for step in range(1, n_chip)
        ]

    def over_col(source, target, send_sem, recv_sem):
        return [
            pltpu.make_async_remote_copy(
                src_ref=source(step), dst_ref=target(step),
                send_sem=send_sem.at[step], recv_sem=recv_sem.at[step],
                device_id=(row, col_peer(step)), device_id_type=mesh_type)
            for step in range(1, n_col)
        ]

    def gather(source, slots, sems):
        send, recv, pass_send, pass_recv = sems
        copies = begin(over_chips(lambda s: source, lambda s: slots(core, chip), send, recv))
        near = begin([to_partner(source, slots(core, chip), pass_send.at[0], pass_recv.at[0])])
        return copies, near

    def relay(state, slots, sems):
        copies, near = state
        send, recv, pass_send, pass_recv = sems
        passed = list(near)
        for step, copy in enumerate(copies, start=1):
            copy.wait_recv()
            here = slots(core, behind(step))
            passed += begin([to_partner(here, here, pass_send.at[step], pass_recv.at[step])])
        return passed

    def gather_sems(index):
        return gs_sem.at[index], gr_sem.at[index], gfs_sem.at[index], gfr_sem.at[index]

    def share_sems(index):
        return as_sem.at[index], ar_sem.at[index], afs_sem.at[index], afr_sem.at[index]

    def fold(part_ref, core_ref, index):
        return begin([to_partner(part_ref.at[other], core_ref, cs_sem.at[index], cr_sem.at[index])])

    def spread(folded, part_ref, core_ref, half_ref, take_ref, index):
        arrive(folded)
        half_ref[...] = (part_ref[core].astype(F32) + core_ref[...].astype(F32)).astype(half_ref.dtype)
        return begin(over_chips(lambda s: half_ref.at[ahead(s)], lambda s: take_ref.at[s],
                                rs_sem.at[index], rr_sem.at[index]))

    def strip_sum(copies, half_ref, take_ref):
        total = half_ref[chip].astype(F32)
        arrive(copies)
        for step in range(1, n_chip):
            total = total + take_ref[step].astype(F32)
        return total

    def put(value, part_ref, at):
        width = value.shape[1]
        part_ref[:, :, :, at : at + width] = value.reshape(part_ref.shape[:3] + (width,))

    def exchange(total, mix_ref, index):
        mix_ref[col] = total
        return begin(over_col(lambda s: mix_ref.at[col], lambda s: mix_ref.at[col],
                              xs_sem.at[index], xr_sem.at[index]))

    def share(copies, mix_ref, full_ref, index):
        arrive(copies)
        total = mix_ref[0]
        for c in range(1, n_col):
            total = total + mix_ref[c]
        full_ref[core, chip] = total
        return gather(full_ref.at[core, chip], lambda k, q: full_ref.at[k, q], share_sems(index))

    def whole(full_ref):
        return full_ref[...].reshape(panel_width, full_ref.shape[3])

    def product(gathered_ref, send_ref):
        right = gathered_ref[...].reshape(n_row * rows_dev, panel_width)

        def run(at, size):
            sums_ref[pl.ds(at, size), :] = dot_nn(dense_ref[pl.ds(at, size), :], right)

        over_chunks(row_blocks * tile, 4 * tile, run)
        for c in range(n_col):
            send_ref[c] = sums_ref[c * rows_dev : (c + 1) * rows_dev, :].astype(BF16)

    def scatter(send_ref, get_ref, index):
        return begin(over_col(lambda s: send_ref.at[col_peer(s)], lambda s: get_ref.at[s],
                              ss_sem.at[index], sr_sem.at[index]))

    def collect(copies, get_ref, result_ref):
        own = sums_ref[pl.ds(pl.multiple_of(col * rows_dev, 8), rows_dev), :]
        arrive(copies)
        for step in range(1, n_col):
            own = own + get_ref[step].astype(F32)
        result_ref[...] = own.astype(BF16)

    def slots_a(k, q):
        return gathered_a.at[q * 2 + k]

    def slots_b(k, q):
        return gathered_b.at[q * 2 + k]

    panel = panel_ref[...]
    put(dot_tn(panel, panel), part_0, 0)
    pl.semaphore_wait(barrier, n_chip + n_col - 1)

    fold_0 = fold(part_0, core_0, 0)
    gather_1 = gather(first_ref, slots_a, gather_sems(0))
    panels = begin(over_col(lambda s: panel_ref, lambda s: panels_ref.at[col], ps_sem, pr_sem))
    gathered_a[row] = first_ref[...]
    panels_ref[col] = panel_ref[...]
    spread_0 = spread(fold_0, part_0, core_0, half_0, take_0, 0)

    load_tiles.wait()
    column_blocks = n_row * rows_dev // tile

    def place(b):
        for j in range(column_blocks):
            slot = jnp.int32(0)
            live = jnp.int32(0)
            for k in range(degree):
                hit = jnp.logical_and(columns_ref[b, k] == j, k < counts_ref[0, b])
                slot = jnp.where(hit, k, slot)
                live = jnp.where(hit, 1, live)
            value = tiles_ref[b, slot]
            dense_ref[pl.ds(b * tile, tile), j * tile : (j + 1) * tile] = jnp.where(
                live > 0, value, jnp.zeros_like(value))

    if row_blocks <= 4:
        for b in range(row_blocks):
            place(b)
    else:
        def place_one(b, carry):
            place(b)
            return carry

        lax.fori_loop(0, row_blocks, place_one, 0)

    passed_1 = relay(gather_1, slots_a, gather_sems(0))
    put(dot_tn(panel, first_ref[...]), part_1, 0)
    fold_1 = fold(part_1, core_1, 1)
    arrive(passed_1)
    product(gathered_a, send_a)
    scatter_1 = scatter(send_a, get_a, 0)

    arrive(panels)
    rows_range = panels_ref[...].reshape(n_col * rows_dev, panel_width).T
    pair = 2 * rows_dev

    def wing(at, size):
        value = dot_nn(rows_range, dense_ref[:, pl.ds(at, size)]).astype(BF16)
        for e in range(size // pair):
            q = at // pair + e
            wing_ref[0, q] = value[:, e * pair : e * pair + rows_dev]
            wing_ref[1, q] = value[:, e * pair + rows_dev : (e + 1) * pair]

    over_chunks(n_row * rows_dev, 8 * rows_dev, wing)
    fold_3 = fold(wing_ref, wing_core, 3)
    exchange_0 = exchange(strip_sum(spread_0, half_0, take_0), mix_0, 0)
    spread_3 = spread(fold_3, wing_ref, wing_core, wing_half, wing_take, 3)
    spread_1 = spread(fold_1, part_1, core_1, half_1, take_1, 1)
    wing_own[...] = strip_sum(spread_3, wing_half, wing_take).astype(BF16)
    share_0 = share(exchange_0, mix_0, full_0, 0)
    collect(scatter_1, get_a, second_ref)
    gather_2 = gather(second_ref, slots_b, gather_sems(1))
    put(dot_tn(panel, second_ref[...]), part_2, 0)
    put(dot_nn(wing_own[...], second_ref[...]), part_2, panel_width)
    fold_2 = fold(part_2, core_2, 2)
    gathered_b[row] = second_ref[...]
    passed_s0 = relay(share_0, lambda k, q: full_0.at[k, q], share_sems(0))
    spread_2 = spread(fold_2, part_2, core_2, half_2, take_2, 2)
    exchange_1 = exchange(strip_sum(spread_1, half_1, take_1), mix_1, 1)
    arrive(passed_s0)

    gram = whole(full_0)
    pieces = 4
    width = panel_width // pieces
    columns = [gram[width * j :, width * j : width * (j + 1)] for j in range(pieces)]
    uppers, inverses, unders = [], [], []

    def factor(b):
        upper, inverse = eliminate(columns[b][:width], work_ref, out_ref)
        under = None
        if b < pieces - 1:
            under = dot_nt(columns[b][width:], inverse, HIGHEST)
            for j in range(b + 1, pieces):
                o = (j - b - 1) * width
                columns[j] = columns[j] - dot_nt(under[o:], under[o : o + width], HIGHEST)
        uppers.append(upper)
        inverses.append(inverse)
        unders.append(under)

    passed_2 = relay(gather_2, slots_b, gather_sems(1))
    factor(0)
    exchange_2 = exchange(strip_sum(spread_2, half_2, take_2), mix_2, 2)
    arrive(passed_2)
    product(gathered_b, send_b)
    scatter_2 = scatter(send_b, get_b, 1)
    share_1 = share(exchange_1, mix_1, full_1, 1)
    factor(1)
    share_2 = share(exchange_2, mix_2, full_2, 2)
    passed_s1 = relay(share_1, lambda k, q: full_1.at[k, q], share_sems(1))
    factor(2)
    passed_s2 = relay(share_2, lambda k, q: full_2.at[k, q], share_sems(2))
    factor(3)

    identity = (lax.broadcasted_iota(jnp.int32, (width, panel_width), 1)
                - lax.broadcasted_iota(jnp.int32, (width, panel_width), 0))
    for b in range(pieces):
        target = (identity == b * width).astype(F32)
        for e in range(b):
            o = (b - e - 1) * width
            target = target - dot_nn(unders[e][o : o + width], lower_ref[e * width : (e + 1) * width, :], HIGHEST)
        lower_ref[b * width : (b + 1) * width, :] = dot_nn(inverses[b], target, HIGHEST)
    for b in range(pieces):
        parts = [jnp.zeros((width, b * width), F32)] if b else []
        parts.append(uppers[b])
        if b < pieces - 1:
            parts.append(unders[b].T)
        upper_out[b * width : (b + 1) * width, :] = jnp.concatenate(parts, axis=1)

    collect(scatter_2, get_b, third_ref)
    arrive(passed_s1)
    cross_out[:, :panel_width] = whole(full_1)
    arrive(passed_s2)
    cross_out[:, panel_width:] = whole(full_2)
    for copy in everything:
        copy.wait_send()


def project(lower_ref, upper_ref, cross_ref, first_ref, second_ref, third_ref, panel_ref,
            upper_out, coef_out, proj_out):
    upper_out[...] = upper_ref[...]
    width = panel_ref.shape[1]
    lower_inverse = lower_ref[...]
    for j, source in enumerate((first_ref, second_ref, third_ref)):
        here = slice(j * width, (j + 1) * width)
        coefficients = dot_nn(lower_inverse, cross_ref[:, here], HIGHEST)
        coef_out[:, here] = coefficients
        weights = dot_tn(lower_inverse, coefficients, HIGHEST)
        weight_high = weights.astype(BF16)
        weight_rest = (weights - weight_high.astype(F32)).astype(BF16)
        removed = dot_nn(panel_ref[...], weight_high) + dot_nn(panel_ref[...], weight_rest)
        proj_out[:, here] = (source[...].astype(F32) - removed).astype(BF16)


def shards(n_row, n_col, sparse_tiles, tile_columns, block_counts, krylov_first, panel_block):
    row_blocks, degree, tile, _ = sparse_tiles.shape
    rows_dev, width = panel_block.shape
    strip = width // n_row
    n_chip = n_row // 2
    vmem = pl.BlockSpec(memory_space=pltpu.VMEM)
    smem = pl.BlockSpec(memory_space=pltpu.SMEM)
    dma = pltpu.SemaphoreType.DMA
    shape = jax.ShapeDtypeStruct
    spans = (1, 1, 2)
    call = pl.pallas_call(
        functools.partial(body, n_row, n_col, degree, row_blocks, tile),
        out_shape=[
            shape((width, width), F32),
            shape((width, width), F32),
            shape((width, 3 * width), F32),
            shape((rows_dev, width), BF16),
            shape((rows_dev, width), BF16),
        ],
        in_specs=[pl.BlockSpec(memory_space=pl.ANY), smem, smem, vmem, vmem],
        out_specs=[vmem] * 5,
        scratch_shapes=[
            pltpu.VMEM(sparse_tiles.shape, BF16),
            pltpu.VMEM((row_blocks * tile, n_row * rows_dev), BF16),
            pltpu.VMEM((n_row, rows_dev, width), BF16),
            pltpu.VMEM((n_row, rows_dev, width), BF16),
            pltpu.VMEM((n_col, rows_dev, width), BF16),
            pltpu.VMEM((row_blocks * tile, width), F32),
            *[pltpu.VMEM((n_col, rows_dev, width), BF16)] * 4,
            pltpu.VMEM((2, n_chip, width, rows_dev), BF16),
            pltpu.VMEM((n_chip, width, rows_dev), BF16),
            pltpu.VMEM((n_chip, width, rows_dev), BF16),
            pltpu.VMEM((n_chip, width, rows_dev), BF16),
            pltpu.VMEM((width, rows_dev), BF16),
            *[pltpu.VMEM((2, n_chip, strip, k * width), F32) for k in spans],
            *[pltpu.VMEM((n_chip, strip, k * width), F32) for k in spans],
            *[pltpu.VMEM((n_chip, strip, k * width), F32) for k in spans],
            *[pltpu.VMEM((n_chip, strip, k * width), F32) for k in spans],
            *[pltpu.VMEM((n_col, strip, k * width), F32) for k in spans],
            *[pltpu.VMEM((2, n_chip, strip, k * width), F32) for k in spans],
            pltpu.VMEM((width // 4, width // 2), F32),
            pltpu.VMEM((width // 4, width // 2), F32),
            dma,
            *[dma((2, n_chip))] * 4,
            *[dma((n_col,))] * 2,
            *[dma((2, n_col))] * 2,
            *[dma((4,))] * 2,
            *[dma((4, n_chip))] * 2,
            *[dma((3, n_col))] * 2,
            *[dma((3, n_chip))] * 4,
        ],
        compiler_params=pltpu.CompilerParams(collective_id=0, has_side_effects=True),
        name="range_finder",
    )
    lower, upper, cross, second, third = call(
        sparse_tiles, tile_columns, block_counts.reshape(1, row_blocks), krylov_first, panel_block
    )
    return tuple(pl.pallas_call(
        project,
        out_shape=[
            shape((width, width), F32),
            shape((width, 3 * width), F32),
            shape((rows_dev, 3 * width), BF16),
        ],
        in_specs=[vmem] * 7,
        out_specs=[vmem] * 3,
        name="project",
    )(lower, upper, cross, krylov_first, second, third, panel_block))


def solution(mesh):
    n_row, n_col = mesh.shape["row"], mesh.shape["col"]
    in_specs = (
        P(("row", "col"), None, None, None),
        P(("row", "col"), None),
        P(("row", "col")),
        P(("row", "col"), None),
        P(("row", "col"), None),
    )
    out_specs = (P(), P(), P(("row", "col"), None))
    return jax.shard_map(
        functools.partial(shards, n_row, n_col), mesh=mesh, in_specs=in_specs, out_specs=out_specs, check_vma=False
    )
```

time: 70.1 us -> 61.5 us (0.88)
  Pallas kernels: 64.8 us -> 60.2 us
  local copies, waits for them, and re-layouts: 4.45 us -> 0 us
    pallas_call x1, Pallas kernels: 64.8 us -> 55.1 us  [shards(): call(sparse_tiles, tile_columns, block_counts.reshape(1, row_blocks), kry...]
    pallas_call x0 -> x1, Pallas kernels: none -> 5.16 us  [shards(): pl.pallas_call(project, out_shape=[shape((width, width), F32), shape((wid...]
    unnamed x5 -> x0, local copies, waits for them, and re-layouts: 4.45 us -> none
where the time goes in v2:
time: 61.5 us; the launch traced here: 60.9 us
  Pallas kernels  60.2 us (98%)
  between operations  0.64 us (1%)
    pallas_call x1, Pallas kernels, shards(): call(sparse_tiles, tile_columns, block_counts.reshape(1, row_blocks), kry...  55.1 us
    pallas_call x1, Pallas kernels, shards(): pl.pallas_call(project, out_shape=[shape((width, width), F32), shape((wid...  5.16 us

profile of v2, /device:TPU:0, one launch (start us, length us, event | category | flops | bytes accessed | tf_op | source)
XLA Modules:
  0.0 60.9 jit_solution(16352891067652463415)
XLA Ops:
  0.6 55.1 %range_finder.1 = (f32[256,256]{1,0:T(8,128)}, f32[256,256]{1,0:T(8,128)}, f32[256,768]{1,0:T(8,128)}, bf16[128,256]{1,0:T(8,128)(2,1)}, bf16[128,256]{1,0:T(8,128)(2,1)}) custom-call(bf16[4,7,128,128]{3,2,1,0:T(8,128)(2,1)} %tiles_hbm.1, s32[4,7]{1,0:T(4,128)} %columns_ref.1, s32[1,4]{1,0:T(1,128)} %bitcast.1, bf16[128,256]{1,0:T(8,128)(2,1)} %first_ref.3, ...), custom_call_target="tpu_custom_call" | custom-call | tf_op jit(solution)/shard_map/range_finder/pallas_call | solution.py:430
  55.7 5.2 %project.1 = (f32[256,256]{1,0:T(8,128)}, f32[256,768]{1,0:T(8,128)}, bf16[128,768]{1,0:T(8,128)(2,1)}) custom-call(f32[256,256]{1,0:T(8,128)} %get-tuple-element.8.lower_ref, f32[256,256]{1,0:T(8,128)} %get-tuple-element.9.upper_ref, f32[256,768]{1,0:T(8,128)} %get-tuple-element.10.cross_ref, bf16[128,256]{1,0:T(8,128)(2,1)} %first_ref.3, ...), custom_call_target="tpu_custom_call" | custom-call | tf_op jit(solution)/shard_map/project/pallas_call | solution.py:433

commit v3 on v2

--- a/solution.py
+++ b/solution.py
@@ -73,9 +73,7 @@
          tiles_hbm, columns_ref, counts_ref, first_ref, panel_ref,
          lower_ref, upper_out, cross_out, second_ref, third_ref,
          tiles_ref, dense_ref, gathered_a, gathered_b, panels_ref, sums_ref, send_a, send_b, get_a, get_b,
-         wing_ref, wing_core, wing_half, wing_take, wing_own,
-         part_0, part_1, part_2, core_0, core_1, core_2, half_0, half_1, half_2, take_0, take_1, take_2,
-         mix_0, mix_1, mix_2, full_0, full_1, full_2,
+         parts, cores, halves, takes, mixes, fulls, turned_ref,
          work_ref, out_ref,
          tile_sem, gs_sem, gr_sem, gfs_sem, gfr_sem, ps_sem, pr_sem, ss_sem, sr_sem,
          cs_sem, cr_sem, rs_sem, rr_sem, xs_sem, xr_sem, as_sem, ar_sem, afs_sem, afr_sem):
@@ -229,16 +227,34 @@
     def slots_b(k, q):
         return gathered_b.at[q * 2 + k]
 
+    def stage(index, value):
+        put(value, parts.at[index], 0)
+        return fold(parts.at[index], cores.at[index], index)
+
+    def spread_stage(index, folded):
+        return spread(folded, parts.at[index], cores.at[index], halves.at[index], takes.at[index], index)
+
+    def exchange_stage(index, copies):
+        return exchange(strip_sum(copies, halves.at[index], takes.at[index]), mixes.at[index], index)
+
+    def full_slots(index):
+        return lambda k, q: fulls.at[index, k, q]
+
+    def share_stage(index, copies):
+        return share(copies, mixes.at[index], fulls.at[index], index)
+
+    def relay_stage(index, state):
+        return relay(state, full_slots(index), share_sems(index))
+
     panel = panel_ref[...]
-    put(dot_tn(panel, panel), part_0, 0)
+    put(dot_tn(panel, panel), parts.at[0], 0)
     pl.semaphore_wait(barrier, n_chip + n_col - 1)
 
-    fold_0 = fold(part_0, core_0, 0)
     gather_1 = gather(first_ref, slots_a, gather_sems(0))
+    fold_0 = fold(parts.at[0], cores.at[0], 0)
     panels = begin(over_col(lambda s: panel_ref, lambda s: panels_ref.at[col], ps_sem, pr_sem))
     gathered_a[row] = first_ref[...]
     panels_ref[col] = panel_ref[...]
-    spread_0 = spread(fold_0, part_0, core_0, half_0, take_0, 0)
 
     load_tiles.wait()
     column_blocks = n_row * rows_dev // tile
@@ -265,43 +281,35 @@
 
         lax.fori_loop(0, row_blocks, place_one, 0)
 
+    spread_0 = spread_stage(0, fold_0)
     passed_1 = relay(gather_1, slots_a, gather_sems(0))
-    put(dot_tn(panel, first_ref[...]), part_1, 0)
-    fold_1 = fold(part_1, core_1, 1)
+    fold_1 = stage(1, dot_tn(panel, first_ref[...]))
     arrive(passed_1)
     product(gathered_a, send_a)
     scatter_1 = scatter(send_a, get_a, 0)
-
-    arrive(panels)
-    rows_range = panels_ref[...].reshape(n_col * rows_dev, panel_width).T
-    pair = 2 * rows_dev
-
-    def wing(at, size):
-        value = dot_nn(rows_range, dense_ref[:, pl.ds(at, size)]).astype(BF16)
-        for e in range(size // pair):
-            q = at // pair + e
-            wing_ref[0, q] = value[:, e * pair : e * pair + rows_dev]
-            wing_ref[1, q] = value[:, e * pair + rows_dev : (e + 1) * pair]
-
-    over_chunks(n_row * rows_dev, 8 * rows_dev, wing)
-    fold_3 = fold(wing_ref, wing_core, 3)
-    exchange_0 = exchange(strip_sum(spread_0, half_0, take_0), mix_0, 0)
-    spread_3 = spread(fold_3, wing_ref, wing_core, wing_half, wing_take, 3)
-    spread_1 = spread(fold_1, part_1, core_1, half_1, take_1, 1)
-    wing_own[...] = strip_sum(spread_3, wing_half, wing_take).astype(BF16)
-    share_0 = share(exchange_0, mix_0, full_0, 0)
+    exchange_0 = exchange_stage(0, spread_0)
+    spread_1 = spread_stage(1, fold_1)
     collect(scatter_1, get_a, second_ref)
     gather_2 = gather(second_ref, slots_b, gather_sems(1))
-    put(dot_tn(panel, second_ref[...]), part_2, 0)
-    put(dot_nn(wing_own[...], second_ref[...]), part_2, panel_width)
-    fold_2 = fold(part_2, core_2, 2)
+    fold_2 = stage(2, dot_tn(panel, second_ref[...]))
     gathered_b[row] = second_ref[...]
-    passed_s0 = relay(share_0, lambda k, q: full_0.at[k, q], share_sems(0))
-    spread_2 = spread(fold_2, part_2, core_2, half_2, take_2, 2)
-    exchange_1 = exchange(strip_sum(spread_1, half_1, take_1), mix_1, 1)
+    exchange_1 = exchange_stage(1, spread_1)
+    share_0 = share_stage(0, exchange_0)
+    spread_2 = spread_stage(2, fold_2)
+    arrive(panels)
+    turned_ref[...] = panels_ref[...].reshape(n_col * rows_dev, panel_width).T
+    passed_2 = relay(gather_2, slots_b, gather_sems(1))
+    exchange_2 = exchange_stage(2, spread_2)
+    passed_s0 = relay_stage(0, share_0)
+    arrive(passed_2)
+    product(gathered_b, send_b)
+    fold_3 = stage(3, dot_nn(turned_ref[...], send_b[...].reshape(n_col * rows_dev, panel_width)))
+    scatter_2 = scatter(send_b, get_b, 1)
+    spread_3 = spread_stage(3, fold_3)
+    share_1 = share_stage(1, exchange_1)
     arrive(passed_s0)
 
-    gram = whole(full_0)
+    gram = whole(fulls.at[0])
     pieces = 4
     width = panel_width // pieces
     columns = [gram[width * j :, width * j : width * (j + 1)] for j in range(pieces)]
@@ -319,18 +327,15 @@
         inverses.append(inverse)
         unders.append(under)
 
-    passed_2 = relay(gather_2, slots_b, gather_sems(1))
     factor(0)
-    exchange_2 = exchange(strip_sum(spread_2, half_2, take_2), mix_2, 2)
-    arrive(passed_2)
-    product(gathered_b, send_b)
-    scatter_2 = scatter(send_b, get_b, 1)
-    share_1 = share(exchange_1, mix_1, full_1, 1)
+    exchange_3 = exchange_stage(3, spread_3)
+    passed_s1 = relay_stage(1, share_1)
+    share_2 = share_stage(2, exchange_2)
     factor(1)
-    share_2 = share(exchange_2, mix_2, full_2, 2)
-    passed_s1 = relay(share_1, lambda k, q: full_1.at[k, q], share_sems(1))
+    share_3 = share_stage(3, exchange_3)
+    passed_s2 = relay_stage(2, share_2)
     factor(2)
-    passed_s2 = relay(share_2, lambda k, q: full_2.at[k, q], share_sems(2))
+    passed_s3 = relay_stage(3, share_3)
     factor(3)
 
     identity = (lax.broadcasted_iota(jnp.int32, (width, panel_width), 1)
@@ -349,28 +354,30 @@
         upper_out[b * width : (b + 1) * width, :] = jnp.concatenate(parts, axis=1)
 
     collect(scatter_2, get_b, third_ref)
-    arrive(passed_s1)
-    cross_out[:, :panel_width] = whole(full_1)
-    arrive(passed_s2)
-    cross_out[:, panel_width:] = whole(full_2)
+    for index, passed in enumerate((passed_s1, passed_s2, passed_s3)):
+        arrive(passed)
+        cross_out[:, index * panel_width : (index + 1) * panel_width] = whole(fulls.at[index + 1])
     for copy in everything:
         copy.wait_send()
 
 
 def project(lower_ref, upper_ref, cross_ref, first_ref, second_ref, third_ref, panel_ref,
             upper_out, coef_out, proj_out):
-    upper_out[...] = upper_ref[...]
-    width = panel_ref.shape[1]
+    block = pl.program_id(0)
+
+    @pl.when(block == 0)
+    def _():
+        upper_out[...] = upper_ref[...]
+
     lower_inverse = lower_ref[...]
-    for j, source in enumerate((first_ref, second_ref, third_ref)):
-        here = slice(j * width, (j + 1) * width)
-        coefficients = dot_nn(lower_inverse, cross_ref[:, here], HIGHEST)
-        coef_out[:, here] = coefficients
-        weights = dot_tn(lower_inverse, coefficients, HIGHEST)
-        weight_high = weights.astype(BF16)
-        weight_rest = (weights - weight_high.astype(F32)).astype(BF16)
-        removed = dot_nn(panel_ref[...], weight_high) + dot_nn(panel_ref[...], weight_rest)
-        proj_out[:, here] = (source[...].astype(F32) - removed).astype(BF16)
+    coefficients = dot_nn(lower_inverse, cross_ref[...], HIGHEST)
+    coef_out[...] = coefficients
+    weights = dot_tn(lower_inverse, coefficients, HIGHEST)
+    weight_high = weights.astype(BF16)
+    weight_rest = (weights - weight_high.astype(F32)).astype(BF16)
+    removed = dot_nn(panel_ref[...], weight_high) + dot_nn(panel_ref[...], weight_rest)
+    source = jnp.where(block == 0, first_ref[...], jnp.where(block == 1, second_ref[...], third_ref[...]))
+    proj_out[...] = (source.astype(F32) - removed).astype(BF16)
 
 
 def shards(n_row, n_col, sparse_tiles, tile_columns, block_counts, krylov_first, panel_block):
@@ -382,7 +389,6 @@
     smem = pl.BlockSpec(memory_space=pltpu.SMEM)
     dma = pltpu.SemaphoreType.DMA
     shape = jax.ShapeDtypeStruct
-    spans = (1, 1, 2)
     call = pl.pallas_call(
         functools.partial(body, n_row, n_col, degree, row_blocks, tile),
         out_shape=[
@@ -402,17 +408,11 @@
             pltpu.VMEM((n_col, rows_dev, width), BF16),
             pltpu.VMEM((row_blocks * tile, width), F32),
             *[pltpu.VMEM((n_col, rows_dev, width), BF16)] * 4,
-            pltpu.VMEM((2, n_chip, width, rows_dev), BF16),
-            pltpu.VMEM((n_chip, width, rows_dev), BF16),
-            pltpu.VMEM((n_chip, width, rows_dev), BF16),
-            pltpu.VMEM((n_chip, width, rows_dev), BF16),
-            pltpu.VMEM((width, rows_dev), BF16),
-            *[pltpu.VMEM((2, n_chip, strip, k * width), F32) for k in spans],
-            *[pltpu.VMEM((n_chip, strip, k * width), F32) for k in spans],
-            *[pltpu.VMEM((n_chip, strip, k * width), F32) for k in spans],
-            *[pltpu.VMEM((n_chip, strip, k * width), F32) for k in spans],
-            *[pltpu.VMEM((n_col, strip, k * width), F32) for k in spans],
-            *[pltpu.VMEM((2, n_chip, strip, k * width), F32) for k in spans],
+            pltpu.VMEM((4, 2, n_chip, strip, width), F32),
+            *[pltpu.VMEM((4, n_chip, strip, width), F32)] * 3,
+            pltpu.VMEM((4, n_col, strip, width), F32),
+            pltpu.VMEM((4, 2, n_chip, strip, width), F32),
+            pltpu.VMEM((width, n_col * rows_dev), BF16),
             pltpu.VMEM((width // 4, width // 2), F32),
             pltpu.VMEM((width // 4, width // 2), F32),
             dma,
@@ -421,8 +421,8 @@
             *[dma((2, n_col))] * 2,
             *[dma((4,))] * 2,
             *[dma((4, n_chip))] * 2,
-            *[dma((3, n_col))] * 2,
-            *[dma((3, n_chip))] * 4,
+            *[dma((4, n_col))] * 2,
+            *[dma((4, n_chip))] * 4,
         ],
         compiler_params=pltpu.CompilerParams(collective_id=0, has_side_effects=True),
         name="range_finder",
@@ -437,8 +437,18 @@
             shape((width, 3 * width), F32),
             shape((rows_dev, 3 * width), BF16),
         ],
-        in_specs=[vmem] * 7,
-        out_specs=[vmem] * 3,
+        grid=(3,),
+        in_specs=[
+            pl.BlockSpec((width, width), lambda j: (0, 0)),
+            pl.BlockSpec((width, width), lambda j: (0, 0)),
+            pl.BlockSpec((width, width), lambda j: (0, j)),
+            *[pl.BlockSpec((rows_dev, width), lambda j: (0, 0))] * 4,
+        ],
+        out_specs=[
+            pl.BlockSpec((width, width), lambda j: (0, 0)),
+            pl.BlockSpec((width, width), lambda j: (0, j)),
+            pl.BlockSpec((rows_dev, width), lambda j: (0, j)),
+        ],
         name="project",
     )(lower, upper, cross, krylov_first, second, third, panel_block))
 

time: 61.5 us -> 60.4 us (0.982)
  Pallas kernels: 60.2 us -> 59.5 us
    pallas_call x1, Pallas kernels: 55.1 us -> 53.9 us  [shards(): call(sparse_tiles, tile_columns, block_counts.reshape(1, row_blocks), kry...]
where the time goes in v3:
time: 60.4 us; the launch traced here: 60.2 us
  Pallas kernels  59.5 us (99%)
  between operations  0.64 us (1%)
    pallas_call x1, Pallas kernels, shards(): call(sparse_tiles, tile_columns, block_counts.reshape(1, row_blocks), kry...  53.9 us
    pallas_call x1, Pallas kernels, shards(): pl.pallas_call(project, out_shape=[shape((width, width), F32), shape((wid...  5.65 us

profile of v3, /device:TPU:0, one launch (start us, length us, event | category | flops | bytes accessed | tf_op | source)
XLA Modules:
  0.0 60.2 jit_solution(14533293690340468438)
XLA Ops:
  0.6 53.9 %range_finder.1 = (f32[256,256]{1,0:T(8,128)}, f32[256,256]{1,0:T(8,128)}, f32[256,768]{1,0:T(8,128)}, bf16[128,256]{1,0:T(8,128)(2,1)}, bf16[128,256]{1,0:T(8,128)(2,1)}) custom-call(bf16[4,7,128,128]{3,2,1,0:T(8,128)(2,1)} %tiles_hbm.1, s32[4,7]{1,0:T(4,128)} %columns_ref.1, s32[1,4]{1,0:T(1,128)} %bitcast.1, bf16[128,256]{1,0:T(8,128)(2,1)} %first_ref.3, ...), custom_call_target="tpu_custom_call" | custom-call | tf_op jit(solution)/shard_map/range_finder/pallas_call | solution.py:430
  54.5 5.7 %project.1 = (f32[256,256]{1,0:T(8,128)}, f32[256,768]{1,0:T(8,128)}, bf16[128,768]{1,0:T(8,128)(2,1)}) custom-call(f32[256,256]{1,0:T(8,128)} %get-tuple-element.8.lower_ref, f32[256,256]{1,0:T(8,128)} %get-tuple-element.9.upper_ref, f32[256,768]{1,0:T(8,128)} %get-tuple-element.10.cross_ref, bf16[128,256]{1,0:T(8,128)(2,1)} %first_ref.3, ...), custom_call_target="tpu_custom_call" | custom-call | tf_op jit(solution)/shard_map/project/pallas_call | solution.py:433
